TPU v7x, 32 devices: a whole 2x2x4 slice. The times are simulated.
32 devices in a mesh: outer: 8 (over z, y), inner: 4 (over x, core).
Axes of the slice: x: 2, y: 2, z: 4, core: 2. Of those that a mesh axis runs over, the one named last changes fastest.
Arguments:
- hidden: bfloat16 [4096, 1024], P(('outer', 'inner')), may hold values from -6 to 6
- x_act: bfloat16 [4096, 2048], P(('outer', 'inner')), may hold values from -6 to 6
- dt_step: float32 [4096, 32], P(('outer', 'inner')), may hold values from 0.00421875 to 0.44, as said below
- log_decay: float32 [4096, 32], P(('outer', 'inner')), may hold values from -0.81 to -7.080078e-06, as said below
- w_bc: bfloat16 [1024, 128], P(('outer', 'inner')), may hold values from -0.1875 to 0.1875
- grad_y: bfloat16 [4096, 2048], P(('outer', 'inner')), may hold values from -0.19921875 to 0.19921875
Outputs:
- grad_x: float32 [4096, 2048], P(('outer', 'inner'))
- grad_hidden: float32 [4096, 1024], P(('outer', 'inner'))
- grad_proj: float32 [1024, 128], P(('outer', 'inner'))
Inputs may be any that keep to these rules, and one draw needn't show every extreme that they name: `dt_step`: Positive; constant in scale within each head apart from a factor within e**-0.5 to e**0.5. `log_decay`: Negative.
All inputs are finite; a program needn't handle non-finite values.
Results may differ from a plain program's by a relative error of at most 0.0029.
Values may be sent and summed in bfloat16 or wider, within the bound.
No kernel may reach another device: no remote copies, remote signals or barrier semaphores. Data moves between devices by JAX's collectives and lax.ppermute only.
A program may use at most 64 MiB of HBM per device.

v0:
```python
import math
import jax
import jax.numpy as jnp
from jax import lax
from jax.sharding import PartitionSpec as P

BLOCK = 128
HIGH = lax.Precision.HIGHEST


def carried_in(array, axis, combine, identity, reverse):
    count, mine = (lax.axis_size(axis), lax.axis_index(axis))
    everything = jax.tree.map(lambda part: lax.all_gather(part, axis), array)
    start = jax.tree.map(
        lambda part, zero: jnp.broadcast_to(jnp.asarray(zero, part.dtype), part.shape),
        array,
        identity,
    )

    def step(k, before):
        at = count - 1 - k if reverse else k
        reached = at > mine if reverse else at < mine
        new = combine(before, jax.tree.map(lambda part: part[at], everything))
        return jax.tree.map(lambda a, b: jnp.where(reached, a, b), new, before)

    return lax.fori_loop(0, count, step, start)


def block_step(carried, pieces):
    inputs, decays, b_rows, c_rows = pieces
    length = inputs.shape[0]
    running = jnp.cumsum(decays, axis=0)
    row_ids = lax.broadcasted_iota(jnp.int32, (length, length), 0)
    col_ids = lax.broadcasted_iota(jnp.int32, (length, length), 1)
    causal = row_ids >= col_ids
    spread = running.T[:, :, None] - running.T[:, None, :]
    segment = jnp.where(causal[None], jnp.exp(jnp.where(causal[None], spread, 0.0)), 0.0)
    scores = jnp.einsum("in,jn->ij", c_rows, b_rows, precision=HIGH)
    outputs = jnp.einsum("hij,jhp->ihp", segment * scores[None], inputs, precision=HIGH)
    outputs = outputs + jnp.exp(running)[:, :, None] * jnp.einsum(
        "in,hpn->ihp", c_rows, carried, precision=HIGH
    )
    final_sum = running[-1]
    weights = jnp.exp(final_sum[None, :] - running)
    updated = jnp.exp(final_sum)[:, None, None] * carried + jnp.einsum(
        "jhp,jn->hpn", inputs * weights[:, :, None], b_rows, precision=HIGH
    )
    return (updated, outputs)


def scan_block(inputs, decays, b_rows, c_rows, carried, length):
    count = inputs.shape[0] // length
    pieces = (
        inputs.reshape((count, length) + inputs.shape[1:]),
        decays.reshape((count, length, decays.shape[1])),
        b_rows.reshape((count, length, b_rows.shape[1])),
        c_rows.reshape((count, length, c_rows.shape[1])),
    )
    final_state, outputs = lax.scan(block_step, carried, pieces)
    return (outputs.reshape(inputs.shape), final_state)


def slice_combine(earlier, later):
    return (earlier[0] + later[0], jnp.exp(later[0])[:, None] * earlier[1] + later[1])


def slice_step(carry, item):
    return (slice_combine(carry, item), carry)


def per_device(hidden, x_act, dt_step, log_decay, w_bc, grad_y):
    weights_full = lax.all_gather(w_bc, ("outer", "inner"), axis=0, tiled=True)
    state_width = weights_full.shape[1] // 2
    row_count = hidden.shape[0]
    head_count = dt_step.shape[1]
    head_size = x_act.shape[1] // head_count
    projected = jnp.dot(hidden, weights_full, preferred_element_type=jnp.float32)
    b_rows = projected[:, :state_width]
    c_rows = projected[:, state_width:]
    inputs = dt_step[:, :, None] * x_act.astype(jnp.float32).reshape(
        row_count, head_count, head_size
    )
    cotangent = grad_y.astype(jnp.float32).reshape(row_count, head_count, head_size)
    running = jnp.cumsum(log_decay, axis=0)
    totals = running[-1]
    own_state = jnp.einsum(
        "jhp,jn->hpn",
        inputs * jnp.exp(totals[None, :] - running)[:, :, None],
        b_rows,
        precision=HIGH,
    )
    own_adjoint = jnp.einsum(
        "ihp,in->hpn", cotangent * jnp.exp(running)[:, :, None], c_rows, precision=HIGH
    )
    inner_count = lax.axis_size("inner")
    flat_width = head_size * state_width
    paired = jnp.stack(
        [own_state.reshape(head_count, flat_width), own_adjoint.reshape(head_count, flat_width)]
    )[None]
    totals_wide = jnp.broadcast_to(totals[None, None, :, None], (1, 1, head_count, inner_count))
    slices, all_totals = (
        lax.all_to_all(paired, "inner", split_axis=3, concat_axis=0, tiled=True),
        lax.all_to_all(totals_wide, "inner", split_axis=3, concat_axis=0, tiled=True),
    )
    all_totals = all_totals[:, 0, :, 0]
    zero_slice = (jnp.zeros((head_count,), jnp.float32), jnp.zeros_like(slices[0, 0]))
    forward_total, forward_prior = lax.scan(slice_step, zero_slice, (all_totals, slices[:, 0]))
    backward_total, backward_after = lax.scan(
        slice_step, zero_slice, (all_totals, slices[:, 1]), reverse=True
    )
    coarse_forward = carried_in(forward_total, "outer", slice_combine, zero_slice, False)
    coarse_backward = carried_in(backward_total, "outer", slice_combine, zero_slice, True)
    state_part = jnp.exp(forward_prior[0])[:, :, None] * coarse_forward[1][None] + forward_prior[1]
    adjoint_part = (
        jnp.exp(backward_after[0])[:, :, None] * coarse_backward[1][None] + backward_after[1]
    )
    returned = lax.all_to_all(
        jnp.stack([state_part, adjoint_part], 1), "inner", split_axis=0, concat_axis=3, tiled=True
    )
    state_in = returned[0, 0].reshape(head_count, head_size, state_width)
    adjoint_out = returned[0, 1].reshape(head_count, head_size, state_width)

    def forward(inputs, b_rows, c_rows):
        return scan_block(inputs, log_decay, b_rows, c_rows, state_in, BLOCK)

    outputs, pullback = jax.vjp(forward, inputs, b_rows, c_rows)
    d_in, d_b, d_c = pullback((cotangent, adjoint_out))
    grad_x = (dt_step[:, :, None] * d_in).reshape(row_count, head_count * head_size)
    d_proj = jnp.concatenate([d_b, d_c], axis=1)
    d_low = d_proj.astype(jnp.bfloat16)
    grad_hidden = lax.dot_general(
        d_low, weights_full, (((1,), (1,)), ((), ())), preferred_element_type=jnp.float32
    )
    scale = 1.0 / math.sqrt(row_count * lax.axis_size("outer") * lax.axis_size("inner"))
    grad_proj = lax.psum_scatter(
        lax.dot_general(hidden, d_low, (((0,), (0,)), ((), ())), preferred_element_type=jnp.float32)
        * scale,
        ("outer", "inner"),
        scatter_dimension=0,
        tiled=True,
    )
    return (grad_x, grad_hidden, grad_proj)


def solution(mesh):
    in_specs = (
        P(("outer", "inner"), None),
        P(("outer", "inner"), None),
        P(("outer", "inner"), None),
        P(("outer", "inner"), None),
        P(("outer", "inner"), None),
        P(("outer", "inner"), None),
    )
    out_specs = (
        P(("outer", "inner"), None),
        P(("outer", "inner"), None),
        P(("outer", "inner"), None),
    )
    return jax.shard_map(
        per_device, mesh=mesh, in_specs=in_specs, out_specs=out_specs, check_vma=False
    )
```

profile of v0, /device:TPU:0, one launch (start us, length us, event | category | flops | bytes accessed | tf_op | source)
XLA Modules:
  0.0 382.8 jit_solution(757989280330233703)
XLA Ops:
  8.3 44.2 %all_gather.27 = bf16[1024,128]{1,0:T(8,128)(2,1)S(1)} all-gather(bf16[32,128]{1,0:T(8,128)(2,1)} %param.18), channel_id=1, replica_groups=mesh['outer'=8,'inner'=4] {'outer','inner'}, dimensions={0}, use_global_device_ids=true | all-gather | bytes 270336 | tf_op jit(solution)/shard_map/all_gather | solution.py:72
  52.5 1.4 copy.64
  57.7 4.4 %copy.68 = f32[2,32,4096]{1,0,2:T(2,128)} copy(f32[2,32,4096]{2,1,0:T(8,128)S(1)} %pad_maximum_fusion) | data formatting | bytes 2097152 | tf_op jit(solution)/shard_map/stack | solution.py:97
  62.1 4.7 %bitcast_bitcast_fusion = f32[4096,1,2,32]{3,2,1,0:T(2,128)} fusion(f32[2,32,4096]{1,0,2:T(2,128)} %copy.68), kind=kLoop, calls=%fused_computation.87 | loop fusion | bytes 2097152
  66.8 6.5 %reshape.273 = f32[4,1,65536]{2,1,0:T(1,128)} reshape(f32[4096,1,2,32]{3,2,1,0:T(2,128)} %bitcast_bitcast_fusion) | data formatting | bytes 2097152
  73.3 4.4 %all-to-all-start.1 = ((f32[4,1,65536]{2,1,0:T(1,128)}), f32[4,1,65536]{2,1,0:T(1,128)}, u32[]{:S(2)}, u32[]{:S(2)}) async-start(f32[4,1,65536]{2,1,0:T(1,128)} %reshape.273), calls=%async_computation.1 | async-start | bytes 2097152 | tf_op jit(solution)/shard_map/all_to_all | solution.py:102
  78.9 13.3 %all-to-all-done.1 = f32[4,1,65536]{2,1,0:T(1,128)} async-done(((f32[4,1,65536]{2,1,0:T(1,128)}), f32[4,1,65536]{2,1,0:T(1,128)}, u32[]{:S(2)}, u32[]{:S(2)}) %all-to-all-start.1) | async-done | bytes 1048608 | tf_op jit(solution)/shard_map/all_to_all | solution.py:102
  92.8 3.8 all-to-all-start
  97.4 4.6 %reduce = f32[4,65536]{1,0:T(4,128)S(1)} reduce(f32[4,1,65536]{2,1,0:T(1,128)} %all-to-all-done.1, f32[]{:T(128)} %broadcast.232), dimensions={1}, to_apply=%all_to_all.40.reduce_sub_computation | reduce | bytes 2097156 | tf_op jit(solution)/shard_map/all_to_all | solution.py:102
  102.0 5.6 %reshape.274 = f32[4096,1,2,32]{3,2,1,0:T(2,128)} reshape(f32[4,65536]{1,0:T(4,128)S(1)} %reduce) | data formatting | bytes 2097152
  107.6 5.3 %copy.86 = f32[1,2,32,4,1024]{4,3,2,1,0:T(4,128)S(1)} copy(f32[1,2,32,4,1024]{2,1,4,3,0:T(2,128)} %bitcast.151) | data formatting | bytes 2097152 | tf_op jit(solution)/shard_map/all_to_all | solution.py:102
  113.8 10.5 %while.88 = (s32[]{:T(128)}, f32[32]{0:T(128)}, f32[32,1024]{1,0:T(8,128)S(1)}, f32[4,32]{1,0:T(4,128)S(1)}, f32[4,32,1024]{2,1,0:T(8,128)S(1)}, /*index=5*/f32[...) while((s32[]{:T(128)}, f32[32]{0:T(128)}, f32[32,1024]{1,0:T(8,128)S(1)}, ...), condition=%wide.region_2.3_spmd.clone, body=%wide.region_1.2_spmd.clone.sunk | while | flops 131139 | bytes 918649 | solution.py:107
  113.9 1.3 fusion.77
  116.5 1.3 fusion.77
  119.1 1.3 fusion.77
  121.7 1.3 fusion.77
  126.1 6.0 %while.90 = (s32[]{:T(128)}, f32[32]{0:T(128)}, f32[32,1024]{1,0:T(8,128)S(1)}, f32[4,32]{1,0:T(4,128)S(1)}, f32[4,32,1024]{2,1,0:T(8,128)S(1)}, /*index=5*/f32[...) while((s32[]{:T(128)}, f32[32]{0:T(128)}, ...), condition=%wide.region_6.7_spmd.clone, body=%wide.region_5.6_spmd.clone.sunk | while | flops 131140 | bytes 918669 | solution.py:108
  126.1 1.2 fusion.80
  132.9 17.3 %all-reduce.2 = (f32[256]{0:T(256)S(1)}, f32[256]{0:T(256)S(1)}) all-reduce(f32[256]{0:T(256)S(1)} %dynamic-update-slice.1, f32[256]{0:T(256)S(1)} %dynamic-update-slice), channel_id=4, replica_groups=mesh['outer'=8,'inner'=4] {'outer'}, use_global_device_ids=true, to_apply=%add.1 | all-reduce | flops 512 | bytes 4096
  150.4 13.0 %all-gather.7.cloned.1.call-done = f32[256,1024]{1,0:T(8,128)} async-done(((f32[32,1024]{1,0:T(8,128)}), f32[256,1024]{1,0:T(8,128)}) %all-gather.7.cloned.1.call-update) | async-done | bytes 1048592 | tf_op jit(solution)/shard_map/all_gather | solution.py:13
  163.3 8.2 %while.89 = (s32[]{:T(128)}, f32[32,1024]{1,0:T(8,128)S(1)}, s32[]{:T(128)}, f32[8,32]{1,0:T(8,128)S(1)}, f32[8,32,1024]{2,1,0:T(8,128)}, /*index=5*/s32[]{:T(128)}, s32[]{:T(128)}) while((s32[]{:T(128)}, f32[32,1024]{1,0:T(8,128)S(1)}, s32[]{:T(128)}, f32[8,32]{1,0:T(8,128)S(1)}, f32[8,32,1024]{2,1,0:T(8,128)}, ...), condition=%wide.region_4.5_spmd.clone, body=%wide.region_3.4_spmd.clone.sunk | while | flops 131076 | bytes 393705 | solution.py:26
  171.6 33.3 %all-gather.9.cloned.1.call-done = f32[256,1024]{1,0:T(8,128)} async-done(((f32[32,1024]{1,0:T(8,128)}), f32[256,1024]{1,0:T(8,128)}) %all-gather.9.cloned.1.call-update) | async-done | bytes 1048592 | tf_op jit(solution)/shard_map/all_gather | solution.py:13
  204.9 8.3 %while.91 = (s32[]{:T(128)}, f32[32,1024]{1,0:T(8,128)S(1)}, s32[]{:T(128)}, f32[8,32]{1,0:T(8,128)S(1)}, f32[8,32,1024]{2,1,0:T(8,128)}, /*index=5*/s32[]{:T(128)}, s32[]{:T(128)}, s32[]{:T(128)}, s32[]{:T(128)}) while((s32[]{:T(128)}, f32[32,1024]{1,0:T(8,128)S(1)}, s32[]{:T(128)}, f32[8,32]{1,0:T(8,128)S(1)}, ...), condition=%wide.region_8.9_spmd.clone, body=%wide.region_7.8_spmd.clone.sunk | while | flops 131080 | bytes 393767 | solution.py:26
  214.5 3.5 all-to-all-start.2
  219.7 3.5 fusion.15
  223.2 2.4 fusion.12
  225.7 6.7 %all-to-all-done.2 = f32[4,2,32,1024]{3,2,1,0:T(8,128)S(1)} async-done(((f32[4,2,32,1024]{3,2,1,0:T(8,128)}), f32[4,2,32,1024]{3,2,1,0:T(8,128)S(1)}, u32[]{:S(2)}, u32[]{:S(2)}) %all-to-all-start.2) | async-done | bytes 1048608 | tf_op jit(solution)/shard_map/all_to_all | solution.py:117
  233.0 2.2 fusion.18
  235.4 1.9 convolution_bitcast_fusion.1
  238.0 3.1 convolution_bitcast_fusion
  242.6 1.3 copy.80
  244.9 131.4 %reduce-scatter.4.cloned.1.call-done = f32[32,128]{1,0:T(8,128)} async-done(((f32[1024,128]{1,0:T(8,128)}), f32[32,128]{1,0:T(8,128)}) %reduce-scatter.4.cloned.1.call-update) | async-done | bytes 16400
  (157 shorter events, 43.1 us)
Async XLA Ops:
  7.2 46.8 %copy-start = (bf16[128,1024]{1,0:T(8,128)(2,1)S(1)}, bf16[128,1024]{1,0:T(8,128)(2,1)}, u32[]{:S(2)}) copy-start(bf16[128,1024]{1,0:T(8,128)(2,1)} %param.14) | copy-start | bytes 786436
  7.2 47.1 %copy-start.8 = (f32[128,32]{0,1:T(8,128)S(1)}, f32[128,32]{0,1:T(8,128)}, u32[]{:S(2)}) copy-start(f32[128,32]{0,1:T(8,128)} %param.16) | copy-start | bytes 49156
  8.2 47.4 %copy-start.13 = (f32[32]{0:T(128)}, f32[32]{0:T(128)S(1)}, u32[]{:S(2)}) copy-start(f32[32]{0:T(128)S(1)} %slice_bitcast_fusion.2) | copy-start | bytes 388
  52.5 1.7 copy-start.3
  53.9 1.7 copy-start.5
  55.7 0.6 copy-start.6
  73.3 4.5 %copy-start.15 = (u32[32]{0:T(128)S(1)}, u32[32]{0:T(128)}, u32[]{:S(2)}) copy-start(u32[32]{0:T(128)} %constant.201) | copy-start | bytes 388
  73.3 18.9 %copy-start.14 = (f32[32]{0:T(128)S(1)}, f32[32]{0:T(128)}, u32[]{:S(2)}) copy-start(f32[32]{0:T(128)} %copy-done.13) | copy-start | bytes 388
  73.3 18.9 %all-to-all-start.1 = ((f32[4,1,65536]{2,1,0:T(1,128)}), f32[4,1,65536]{2,1,0:T(1,128)}, u32[]{:S(2)}, u32[]{:S(2)}) async-start(f32[4,1,65536]{2,1,0:T(1,128)} %reshape.273), calls=%async_computation.1 | async-start | bytes 2097152 | tf_op jit(solution)/shard_map/all_to_all | solution.py:102
  92.8 21.0 %all-to-all-start = ((f32[1,1,32,4]{2,1,0,3:T(1,128)}), f32[1,1,32,4]{2,1,0,3:T(1,128)}, u32[]{:S(2)}, u32[]{:S(2)}) async-start(f32[1,1,32,4]{2,1,0,3:T(1,128)} %broadcast_in_dim.120), calls=%async_computation | async-start | bytes 4096 | tf_op jit(solution)/shard_map/all_to_all | solution.py:103
  96.6 66.7 %all-gather.7.cloned.1.call-start = ((), (), s32[]{:S(2)}) async-start(), calls=%async_computation.4 | async-start | bytes 1179648 | tf_op jit(solution)/shard_map/all_gather | solution.py:13
  124.4 0.7 copy-start.2
  124.4 1.6 copy-start.11
  125.0 79.9 %all-gather.9.cloned.1.call-start = ((), (), s32[]{:S(2)}) async-start(), calls=%async_computation.5 | async-start | bytes 1179648 | tf_op jit(solution)/shard_map/all_gather | solution.py:13
  126.0 24.3 %copy-start.12 = (f32[4,32]{1,0:T(4,128)S(1)}, f32[4,32]{1,0:T(4,128)}, u32[]{:S(2)}) copy-start(f32[4,32]{1,0:T(4,128)} %copy-done.11) | copy-start | bytes 1540
  132.1 18.3 %copy-start.1 = (f32[32,1024]{1,0:T(8,128)}, f32[32,1024]{1,0:T(8,128)S(1)}, u32[]{:S(2)}) copy-start(f32[32,1024]{1,0:T(8,128)S(1)} %get-tuple-element.577) | copy-start | bytes 393220
  213.4 4.9 %copy-start.7 = (f32[128,32]{0,1:T(8,128)S(1)}, f32[128,32]{0,1:T(8,128)}, u32[]{:S(2)}) copy-start(f32[128,32]{0,1:T(8,128)} %copy-done.6) | copy-start | bytes 49156
  214.5 17.9 %all-to-all-start.2 = ((f32[4,2,32,1024]{3,2,1,0:T(8,128)}), f32[4,2,32,1024]{3,2,1,0:T(8,128)S(1)}, u32[]{:S(2)}, u32[]{:S(2)}) async-start(f32[4,2,32,1024]{3,2,1,0:T(8,128)} %pad_maximum_fusion.1), calls=%async_computation.2 | async-start | bytes 2097152 | tf_op jit(solution)/shard_map/all_to_all | solution.py:117
  218.0 158.3 %reduce-scatter.4.cloned.1.call-start = ((), (), s32[]{:S(2)}) async-start(), calls=%async_computation.6 | async-start | bytes 540672
  219.7 3.5 copy-start.9
  233.0 2.3 copy-start.10
  241.3 2.6 copy-start.4
Sparse Core Ops, SparseCore 0:
  125.2 38.1 all-gather.6
  166.0 38.8 all-gather.8
  242.7 133.5 reduce-scatter.3
where the time goes:
time: 384 us; the launch traced here: 383 us
  waiting for transfers between devices  198 us (52%)
  blocking collectives  61.5 us (16%)
  local copies, waits for them, and re-layouts  44.6 us (12%)
  other arithmetic  34 us (9%)
  matrix products  17.4 us (5%)
  between operations  14.8 us (4%)
  starting transfers between devices  12.3 us (3%)
    unnamed x4, waiting for transfers between devices  131 us
    all_gather x2, waiting for transfers between devices, carried_in(): everything = jax.tree.map(lambda part: lax.all_gather(part, axis), array)  46.3 us
    all_gather x1, blocking collectives, per_device(): weights_full = lax.all_gather(w_bc, ('outer', 'inner'), axis=0, tiled=True)  44.2 us
    unnamed x45, local copies, waits for them, and re-layouts  25 us
    unnamed x1, blocking collectives  17.3 us
    select_n x16, other arithmetic, step(): return jax.tree.map(lambda a, b: jnp.where(reached, a, b), new, before)  15.9 us
    all_to_all x1, waiting for transfers between devices, per_device(): lax.all_to_all(paired, 'inner', split_axis=3, concat_axis=0, tiled=True)  13.3 us
    exp x8, other arithmetic, slice_combine(): jnp.exp(later[0])[:, None] * earlier[1] + later[1]  9.94 us
  transfers between devices with their start and end apart: 6, of which 5 were waited for; matrix products, arithmetic and copies ran while one was open for 11% of the time, Pallas kernels for 0%

commit v1 on v0

--- a/solution.py
+++ b/solution.py
@@ -6,6 +6,14 @@
 
 BLOCK = 128
 HIGH = lax.Precision.HIGHEST
+
+
+def _show_rounds(net_axis, payload):
+    right_arr = lax.axis_size(net_axis)
+    z2 = jnp.split(payload, right_arr, axis=3)
+    after = jnp.stack(z2, axis=0)
+    q_next = lax.all_to_all(after, net_axis, 0, 0)
+    return jnp.concatenate(q_next, axis=0)
 
 
 def carried_in(array, axis, combine, identity, reverse):
@@ -99,7 +107,7 @@
     )[None]
     totals_wide = jnp.broadcast_to(totals[None, None, :, None], (1, 1, head_count, inner_count))
     slices, all_totals = (
-        lax.all_to_all(paired, "inner", split_axis=3, concat_axis=0, tiled=True),
+        _show_rounds("inner", paired),
         lax.all_to_all(totals_wide, "inner", split_axis=3, concat_axis=0, tiled=True),
     )
     all_totals = all_totals[:, 0, :, 0]

time: 384 us -> 353 us (0.919)
  local copies, waits for them, and re-layouts: 44.6 us -> 13.4 us
    unnamed x45 -> x46, local copies, waits for them, and re-layouts: 25 us -> 8.31 us
    all_to_all x2 -> x0, local copies, waits for them, and re-layouts: 5.84 us -> none  [per_device(): lax.all_to_all(paired, 'inner', split_axis=3, concat_axis=0, tiled=True)]
    dynamic_slice x8 -> x0, local copies, waits for them, and re-layouts: 5.31 us -> none  [per_device(): lax.scan(slice_step, zero_slice, (all_totals, slices[:, 0]))]
    all_to_all x1 -> x0, other arithmetic: 4.61 us -> none  [per_device(): lax.all_to_all(paired, 'inner', split_axis=3, concat_axis=0, tiled=True)]
    another operation x3 -> x2, local copies, waits for them, and re-layouts: 5.13 us -> 0.72 us  [per_device(): jnp.stack([own_state.reshape(head_count, flat_width), own_adjoint.reshape...]
  transfers between devices with their start and end apart: 6 -> 6, of which waited for: 5 -> 6; matrix products, arithmetic and copies ran while one was open for 11% -> 8% of each run, Pallas kernels for 0% -> 0%
where the time goes in v1:
time: 353 us; the launch traced here: 352 us
  waiting for transfers between devices  199 us (56%)
  blocking collectives  61.4 us (17%)
  other arithmetic  33.9 us (10%)
  matrix products  17.4 us (5%)
  between operations  14.9 us (4%)
  local copies, waits for them, and re-layouts  13.4 us (4%)
  starting transfers between devices  11.4 us (3%)
    unnamed x4, waiting for transfers between devices  131 us
    all_gather x2, waiting for transfers between devices, carried_in(): everything = jax.tree.map(lambda part: lax.all_gather(part, axis), array)  45.1 us
    all_gather x1, blocking collectives, per_device(): weights_full = lax.all_gather(w_bc, ('outer', 'inner'), axis=0, tiled=True)  44.2 us
    unnamed x1, blocking collectives  17.2 us
    select_n x16, other arithmetic, step(): return jax.tree.map(lambda a, b: jnp.where(reached, a, b), new, before)  15.9 us
    all_to_all x1, waiting for transfers between devices, _show_rounds(): q_next = lax.all_to_all(after, net_axis, 0, 0)  13.1 us
    exp x8, other arithmetic, slice_combine(): jnp.exp(later[0])[:, None] * earlier[1] + later[1]  9.85 us
    unnamed x46, local copies, waits for them, and re-layouts  8.31 us
  transfers between devices with their start and end apart: 6, of which 6 were waited for; matrix products, arithmetic and copies ran while one was open for 8% of the time, Pallas kernels for 0%

profile of v1, /device:TPU:0, one launch (start us, length us, event | category | flops | bytes accessed | tf_op | source)
XLA Modules:
  0.0 352.2 jit_solution(10642059735456077125)
XLA Ops:
  8.8 44.2 %all_gather.27 = bf16[1024,128]{1,0:T(8,128)(2,1)S(1)} all-gather(bf16[32,128]{1,0:T(8,128)(2,1)} %param.18), channel_id=1, replica_groups=mesh['outer'=8,'inner'=4] {'outer','inner'}, dimensions={0}, use_global_device_ids=true | all-gather | bytes 270336 | tf_op jit(solution)/shard_map/all_gather | solution.py:80
  58.9 3.6 %all-to-all-start.1 = ((f32[4,1,2,32,1024]{4,3,2,1,0:T(8,128)}), f32[4,1,2,32,1024]{4,3,2,1,0:T(8,128)S(1)}, u32[]{:S(2)}, u32[]{:S(2)}) async-start(f32[4,1,2,32,1024]{4,3,2,1,0:T(8,128)} %pad_maximum_fusion), calls=%async_computation.1 | async-start | bytes 2097152 | tf_op jit(solution)/shard_map/all_to_all | solution.py:15
  63.9 13.1 %all-to-all-done.1 = f32[4,1,2,32,1024]{4,3,2,1,0:T(8,128)S(1)} async-done(((f32[4,1,2,32,1024]{4,3,2,1,0:T(8,128)}), f32[4,1,2,32,1024]{4,3,2,1,0:T(8,128)S(1)}, u32[]{:S(2)}, u32[]{:S(2)}) %all-to-all-start.1) | async-done | bytes 1048608 | tf_op jit(solution)/shard_map/all_to_all | solution.py:15
  77.5 3.8 %all-to-all-start = ((f32[1,1,32,4]{2,1,0,3:T(1,128)}), f32[1,1,32,4]{2,1,0,3:T(1,128)}, u32[]{:S(2)}, u32[]{:S(2)}) async-start(f32[1,1,32,4]{2,1,0,3:T(1,128)} %broadcast_in_dim.120), calls=%async_computation | async-start | bytes 4096 | tf_op jit(solution)/shard_map/all_to_all | solution.py:111
  82.3 2.8 all-to-all-done
  85.2 9.3 %while.88 = (s32[]{:T(128)}, f32[32]{0:T(128)}, f32[32,1024]{1,0:T(8,128)S(1)}, f32[4,32]{1,0:T(4,128)S(1)}, f32[4,32,1024]{2,1,0:T(8,128)S(1)}, /*index=5*/f32[...) while((s32[]{:T(128)}, f32[32]{0:T(128)}, f32[32,1024]{1,0:T(8,128)S(1)}, ...), condition=%wide.region_2.3_spmd.clone, body=%wide.region_1.2_spmd.clone.sunk | while | flops 131139 | bytes 656505 | solution.py:115
  85.2 1.3 fusion.73
  87.5 1.3 fusion.73
  89.8 1.3 fusion.73
  92.1 1.3 fusion.73
  96.1 5.4 %while.90 = (s32[]{:T(128)}, f32[32]{0:T(128)}, f32[32,1024]{1,0:T(8,128)S(1)}, f32[4,32]{1,0:T(4,128)S(1)}, f32[4,32,1024]{2,1,0:T(8,128)S(1)}, /*index=5*/f32[...) while((s32[]{:T(128)}, f32[32]{0:T(128)}, ...), condition=%wide.region_6.7_spmd.clone, body=%wide.region_5.6_spmd.clone.sunk | while | flops 131140 | bytes 656525 | solution.py:116
  96.1 1.2 fusion.75
  97.5 1.2 fusion.75
  98.9 1.2 fusion.75
  100.2 1.2 fusion.75
  102.4 17.2 %all-reduce.2 = (f32[256]{0:T(256)S(1)}, f32[256]{0:T(256)S(1)}) all-reduce(f32[256]{0:T(256)S(1)} %dynamic-update-slice.1, f32[256]{0:T(256)S(1)} %dynamic-update-slice), channel_id=4, replica_groups=mesh['outer'=8,'inner'=4] {'outer'}, use_global_device_ids=true, to_apply=%add.1 | all-reduce | flops 512 | bytes 4096
  119.9 11.6 %all-gather.7.cloned.1.call-done = f32[256,1024]{1,0:T(8,128)} async-done(((f32[32,1024]{1,0:T(8,128)}), f32[256,1024]{1,0:T(8,128)}) %all-gather.7.cloned.1.call-update) | async-done | bytes 1048592 | tf_op jit(solution)/shard_map/all_gather | solution.py:21
  131.5 8.2 %while.89 = (s32[]{:T(128)}, f32[32,1024]{1,0:T(8,128)S(1)}, s32[]{:T(128)}, f32[8,32]{1,0:T(8,128)S(1)}, f32[8,32,1024]{2,1,0:T(8,128)}, /*index=5*/s32[]{:T(128)}, s32[]{:T(128)}) while((s32[]{:T(128)}, f32[32,1024]{1,0:T(8,128)S(1)}, s32[]{:T(128)}, f32[8,32]{1,0:T(8,128)S(1)}, f32[8,32,1024]{2,1,0:T(8,128)}, ...), condition=%wide.region_4.5_spmd.clone, body=%wide.region_3.4_spmd.clone.sunk | while | flops 131076 | bytes 393705 | solution.py:34
  139.7 33.5 %all-gather.9.cloned.1.call-done = f32[256,1024]{1,0:T(8,128)} async-done(((f32[32,1024]{1,0:T(8,128)}), f32[256,1024]{1,0:T(8,128)}) %all-gather.9.cloned.1.call-update) | async-done | bytes 1048592 | tf_op jit(solution)/shard_map/all_gather | solution.py:21
  173.2 8.3 %while.91 = (s32[]{:T(128)}, f32[32,1024]{1,0:T(8,128)S(1)}, s32[]{:T(128)}, f32[8,32]{1,0:T(8,128)S(1)}, f32[8,32,1024]{2,1,0:T(8,128)}, /*index=5*/s32[]{:T(128)}, s32[]{:T(128)}, s32[]{:T(128)}, s32[]{:T(128)}) while((s32[]{:T(128)}, f32[32,1024]{1,0:T(8,128)S(1)}, s32[]{:T(128)}, f32[8,32]{1,0:T(8,128)S(1)}, ...), condition=%wide.region_8.9_spmd.clone, body=%wide.region_7.8_spmd.clone.sunk | while | flops 131080 | bytes 393767 | solution.py:34
  181.7 1.1 pad_maximum_fusion.1
  182.8 3.6 %all-to-all-start.2 = ((f32[4,2,32,1024]{3,2,1,0:T(8,128)}), f32[4,2,32,1024]{3,2,1,0:T(8,128)S(1)}, u32[]{:S(2)}, u32[]{:S(2)}) async-start(f32[4,2,32,1024]{3,2,1,0:T(8,128)} %pad_maximum_fusion.1), calls=%async_computation.2 | async-start | bytes 2097152 | tf_op jit(solution)/shard_map/all_to_all | solution.py:125
  188.1 3.5 fusion.13
  191.6 2.4 fusion.10
  194.1 6.8 %all-to-all-done.2 = f32[4,2,32,1024]{3,2,1,0:T(8,128)S(1)} async-done(((f32[4,2,32,1024]{3,2,1,0:T(8,128)}), f32[4,2,32,1024]{3,2,1,0:T(8,128)S(1)}, u32[]{:S(2)}, u32[]{:S(2)}) %all-to-all-start.2) | async-done | bytes 1048608 | tf_op jit(solution)/shard_map/all_to_all | solution.py:125
  201.4 2.2 fusion.16
  203.9 1.9 convolution_bitcast_fusion.1
  205.8 1.4 squeeze.114
  207.4 3.1 convolution_bitcast_fusion
  212.0 1.3 copy.60
  213.3 1.0 fusion.47
  214.3 131.4 %reduce-scatter.4.cloned.1.call-done = f32[32,128]{1,0:T(8,128)} async-done(((f32[1024,128]{1,0:T(8,128)}), f32[32,128]{1,0:T(8,128)}) %reduce-scatter.4.cloned.1.call-update) | async-done | bytes 16400
  (148 shorter events, 37.2 us)
Async XLA Ops:
  7.2 46.1 %copy-start = (bf16[128,1024]{1,0:T(8,128)(2,1)S(1)}, bf16[128,1024]{1,0:T(8,128)(2,1)}, u32[]{:S(2)}) copy-start(bf16[128,1024]{1,0:T(8,128)(2,1)} %param.14) | copy-start | bytes 786436
  7.2 45.8 %copy-start.6 = (bf16[128,2048]{1,0:T(8,128)(2,1)S(1)}, bf16[128,2048]{1,0:T(8,128)(2,1)}, u32[]{:S(2)}) copy-start(bf16[128,2048]{1,0:T(8,128)(2,1)} %param.15) | copy-start | bytes 1572868
  8.3 0.5 copy-start.15
  8.3 45.5 %copy-start.10 = (f32[128,32]{0,1:T(8,128)S(1)}, f32[128,32]{0,1:T(8,128)}, u32[]{:S(2)}) copy-start(f32[128,32]{0,1:T(8,128)} %param.16) | copy-start | bytes 49156
  53.0 0.7 copy-start.4
  54.7 1.0 copy-start.7
  55.8 0.6 copy-start.8
  58.9 3.7 %copy-start.17 = (u32[32]{0:T(128)S(1)}, u32[32]{0:T(128)}, u32[]{:S(2)}) copy-start(u32[32]{0:T(128)} %constant.201) | copy-start | bytes 388
  58.9 18.1 %copy-start.16 = (f32[32]{0:T(128)S(1)}, f32[32]{0:T(128)}, u32[]{:S(2)}) copy-start(f32[32]{0:T(128)} %copy-done.15) | copy-start | bytes 388
  58.9 18.1 %all-to-all-start.1 = ((f32[4,1,2,32,1024]{4,3,2,1,0:T(8,128)}), f32[4,1,2,32,1024]{4,3,2,1,0:T(8,128)S(1)}, u32[]{:S(2)}, u32[]{:S(2)}) async-start(f32[4,1,2,32,1024]{4,3,2,1,0:T(8,128)} %pad_maximum_fusion), calls=%async_computation.1 | async-start | bytes 2097152 | tf_op jit(solution)/shard_map/all_to_all | solution.py:15
  77.5 7.6 %all-to-all-start = ((f32[1,1,32,4]{2,1,0,3:T(1,128)}), f32[1,1,32,4]{2,1,0,3:T(1,128)}, u32[]{:S(2)}, u32[]{:S(2)}) async-start(f32[1,1,32,4]{2,1,0,3:T(1,128)} %broadcast_in_dim.120), calls=%async_computation | async-start | bytes 4096 | tf_op jit(solution)/shard_map/all_to_all | solution.py:111
  81.4 50.1 %all-gather.7.cloned.1.call-start = ((), (), s32[]{:S(2)}) async-start(), calls=%async_computation.4 | async-start | bytes 1179648 | tf_op jit(solution)/shard_map/all_gather | solution.py:21
  94.4 0.7 copy-start.2
  94.5 1.6 copy-start.13
  95.1 78.1 %all-gather.9.cloned.1.call-start = ((), (), s32[]{:S(2)}) async-start(), calls=%async_computation.5 | async-start | bytes 1179648 | tf_op jit(solution)/shard_map/all_gather | solution.py:21
  96.1 23.7 %copy-start.14 = (f32[4,32]{1,0:T(4,128)S(1)}, f32[4,32]{1,0:T(4,128)}, u32[]{:S(2)}) copy-start(f32[4,32]{1,0:T(4,128)} %copy-done.13) | copy-start | bytes 1540
  101.6 18.3 %copy-start.1 = (f32[32,1024]{1,0:T(8,128)}, f32[32,1024]{1,0:T(8,128)S(1)}, u32[]{:S(2)}) copy-start(f32[32,1024]{1,0:T(8,128)S(1)} %get-tuple-element.577) | copy-start | bytes 393220
  182.8 3.9 %copy-start.9 = (f32[128,32]{0,1:T(8,128)S(1)}, f32[128,32]{0,1:T(8,128)}, u32[]{:S(2)}) copy-start(f32[128,32]{0,1:T(8,128)} %copy-done.8) | copy-start | bytes 49156
  182.8 18.1 %all-to-all-start.2 = ((f32[4,2,32,1024]{3,2,1,0:T(8,128)}), f32[4,2,32,1024]{3,2,1,0:T(8,128)S(1)}, u32[]{:S(2)}, u32[]{:S(2)}) async-start(f32[4,2,32,1024]{3,2,1,0:T(8,128)} %pad_maximum_fusion.1), calls=%async_computation.2 | async-start | bytes 2097152 | tf_op jit(solution)/shard_map/all_to_all | solution.py:125
  186.4 159.3 %reduce-scatter.4.cloned.1.call-start = ((), (), s32[]{:S(2)}) async-start(), calls=%async_computation.6 | async-start | bytes 540672
  188.1 3.5 %copy-start.11 = (f32[128,32]{0,1:T(8,128)S(1)}, f32[128,32]{0,1:T(8,128)}, u32[]{:S(2)}) copy-start(f32[128,32]{0,1:T(8,128)} %param.16) | copy-start | bytes 49156
  201.4 2.3 copy-start.12
  205.8 1.7 copy-start.3
  212.0 1.3 copy-start.5
Sparse Core Ops, SparseCore 0:
  95.2 36.2 all-gather.6
  134.2 38.9 all-gather.8
  212.1 133.5 reduce-scatter.3
